TPU v7x, 32 devices: a whole 2x2x4 slice. The times are simulated.
32 devices in a mesh: dp: 2 (over y), row: 4 (over x, core), col: 4 (over z).
Axes of the slice: x: 2, y: 2, z: 4, core: 2. Of those that a mesh axis runs over, the one named last changes fastest.
Arguments:
- tokens: bfloat16 [2048, 4096], P(('col', 'row'), 'dp'), may hold values from -6 to 6
- segments: int32 [4096], P('dp'), may hold values from 0 to 12, never falling along the last dimension, each value on 1 to 800 neighbouring positions
- channel_table: bfloat16 [14, 2048], P(None, ('col', 'row')), may hold values from -7.6 to 2
- w_recept: bfloat16 [4, 512, 2048], P(None, 'row', 'col'), may hold values from -0.125 to 0.125
- w_key: bfloat16 [4, 512, 2048], P(None, 'row', 'col'), may hold values from -0.125 to 0.125
- w_value: bfloat16 [4, 512, 2048], P(None, 'row', 'col'), may hold values from -0.125 to 0.125
- w_gate: bfloat16 [4, 512, 2048], P(None, 'row', 'col'), may hold values from -0.125 to 0.125
- w_output: bfloat16 [4, 512, 2048], P(None, 'row', 'col'), may hold values from -0.125 to 0.125
- ffn_key: bfloat16 [4, 1792, 2048], P(None, 'row', 'col'), may hold values from -0.125 to 0.125
- ffn_value: bfloat16 [4, 512, 7168], P(None, 'row', 'col'), may hold values from -0.0625 to 0.0625
- ffn_recept: bfloat16 [4, 512, 2048], P(None, 'row', 'col'), may hold values from -0.125 to 0.125
- cotangent: bfloat16 [2048, 4096], P(('col', 'row'), 'dp'), may hold values from -6 to 6
Outputs:
- mixed: bfloat16 [2048, 4096], P(('col', 'row'), 'dp')
- grad_tokens: float32 [2048, 4096], P(('col', 'row'), 'dp')
- grad_table: float32 [14, 2048], P(None, ('col', 'row'))
- grad_recept: float32 [4, 512, 2048], P(None, 'row', 'col')
- grad_key: float32 [4, 512, 2048], P(None, 'row', 'col')
- grad_value: float32 [4, 512, 2048], P(None, 'row', 'col')
- grad_gate: float32 [4, 512, 2048], P(None, 'row', 'col')
- grad_output: float32 [4, 512, 2048], P(None, 'row', 'col')
- grad_ffn_key: float32 [4, 1792, 2048], P(None, 'row', 'col')
- grad_ffn_value: float32 [4, 512, 7168], P(None, 'row', 'col')
- grad_ffn_recept: float32 [4, 512, 2048], P(None, 'row', 'col')
Inputs may be any that keep to these rules, and one draw needn't show every extreme that they name: `segments`: numbers never fall along the tokens; each document holds 1 to 800 tokens and one holds exactly 800; a document may run past a sequence's end.
All inputs are finite; a program needn't handle non-finite values.
Results may differ from a plain program's by a relative error of at most 0.019.
Values may be sent and summed in bfloat16 or wider, within the bound.
No kernel may reach another device: no remote copies, remote signals or barrier semaphores. Data moves between devices by JAX's collectives and lax.ppermute only.
A program may use at most 192 MiB of HBM per device.

v0:
```python
import jax
import jax.numpy as jnp
from jax import lax
from jax.sharding import PartitionSpec as P

D = 2048
CHANNELS_PER_ATTN = 64
SEQ = 1024
exact_mode = lax.Precision.HIGHEST
norm_eps = 1e-05
group_eps = 0.00064
head_divisor = 8.0
block_len = 64


def feature_sums(stacked):
    return lax.psum(stacked, ("row", "col"))


def norm_forward(payload_entries, gain, bias):
    center = feature_sums(jnp.sum(payload_entries, axis=1)[None])[0] / D
    spread = (
        feature_sums(jnp.sum(jnp.square(payload_entries - center[:, None]), axis=1)[None])[0] / D
    )
    inverse = lax.rsqrt(spread + norm_eps)
    unit_normal = (payload_entries - center[:, None]) * inverse[:, None]
    return (unit_normal * gain + bias, unit_normal, inverse)


def norm_backward(grad_out, unit_normal, inverse, gain):
    grad_unit = grad_out * gain
    totals = feature_sums(
        jnp.stack([jnp.sum(grad_unit, axis=1), jnp.sum(grad_unit * unit_normal, axis=1)])
    )
    grad_in = inverse[:, None] * (
        grad_unit - totals[0][:, None] / D - unit_normal * totals[1][:, None] / D
    )
    return (grad_in, jnp.sum(grad_out * unit_normal, axis=0), jnp.sum(grad_out, axis=0))


def shift_down(payload_entries, handed_onward):
    earlier = jnp.concatenate([jnp.zeros_like(payload_entries[:1]), payload_entries[:-1]], axis=0)
    return earlier * handed_onward[:, None]


def mix_inputs(normed, coeffs, handed_onward):
    shifted = shift_down(normed, handed_onward)
    return normed[None] * coeffs[:, None, :] + shifted[None] * (1.0 - coeffs[:, None, :])


def attention_mixing_segmented(
    ongoing_memory_matrix, segment_portions, logarithmic_fading_speed, extra_current_coeffs
):
    acceptance_entries, lookup_sources, payload_entries, beginning_markers = segment_portions
    positions = jnp.arange(block_len, dtype=jnp.int32)
    start_marks = jnp.where(beginning_markers > 0.5, positions, -1)
    last_start = lax.cummax(start_marks, axis=0)
    steps_in = positions.astype(jnp.float32)[:, None, None]
    scaled_r = acceptance_entries * jnp.exp(logarithmic_fading_speed[None] * steps_in)
    scaled_k = lookup_sources * jnp.exp(-logarithmic_fading_speed[None] * (steps_in + 1.0))
    end_k = lookup_sources * jnp.exp(logarithmic_fading_speed[None] * (block_len - 1.0 - steps_in))
    allowed = (positions[:, None] > positions[None, :]) & (
        last_start[:, None] <= positions[None, :]
    )
    scores = jnp.einsum("thi,shi->hts", scaled_r, scaled_k, precision=exact_mode)
    scores = jnp.where(allowed[None], scores, 0.0)
    intra_term = jnp.einsum("hts,shj->thj", scores, payload_entries, precision=exact_mode)
    diagonal_contribution = (
        jnp.sum(
            acceptance_entries * extra_current_coeffs[None] * lookup_sources, axis=2, keepdims=True
        )
        * payload_entries
    )
    open_start = (last_start < 0).astype(jnp.float32)
    inter_term = (
        jnp.einsum("thi,hij->thj", scaled_r, ongoing_memory_matrix, precision=exact_mode)
        * open_start[:, None, None]
    )
    tail_mask = (positions >= last_start[block_len - 1]).astype(jnp.float32)
    fresh_sum = jnp.einsum(
        "shi,shj->hij", end_k * tail_mask[:, None, None], payload_entries, precision=exact_mode
    )
    carried = (
        ongoing_memory_matrix
        * jnp.exp(logarithmic_fading_speed * block_len)[:, :, None]
        * open_start[block_len - 1]
        + fresh_sum
    )
    return (carried, intra_term + diagonal_contribution + inter_term)


def attention_mixing_complete(
    acceptance_entries,
    lookup_sources,
    payload_entries,
    beginning_markers,
    logarithmic_fading_speed,
    extra_current_coeffs,
):
    block_count = acceptance_entries.shape[0] // block_len

    def reshaped(array_in):
        return array_in.reshape((block_count, block_len) + array_in.shape[1:])

    checked_outcome = jax.checkpoint(attention_mixing_segmented)

    def step_fn(ongoing_memory_matrix, segment_portions):
        return checked_outcome(
            ongoing_memory_matrix, segment_portions, logarithmic_fading_speed, extra_current_coeffs
        )

    initial = jnp.zeros(
        (
            logarithmic_fading_speed.shape[0],
            logarithmic_fading_speed.shape[1],
            logarithmic_fading_speed.shape[1],
        ),
        jnp.float32,
    )
    unused, outputs = lax.scan(
        step_fn,
        initial,
        (
            reshaped(acceptance_entries),
            reshaped(lookup_sources),
            reshaped(payload_entries),
            reshaped(beginning_markers),
        ),
    )
    return outputs.reshape(acceptance_entries.shape)


def time_block(projected, incoming_entries, handed_onward):
    unit_width = projected.shape[1] // 4
    attention_group_total = unit_width // CHANNELS_PER_ATTN
    token_count = projected.shape[0]

    def divide_attention_groups(array_in):
        return array_in.reshape(token_count, attention_group_total, CHANNELS_PER_ATTN)

    acceptance_entries = divide_attention_groups(projected[:, :unit_width])
    lookup_sources = divide_attention_groups(projected[:, unit_width : 2 * unit_width])
    payload_entries = divide_attention_groups(projected[:, 2 * unit_width : 3 * unit_width])
    gate_pre = projected[:, 3 * unit_width :]
    logarithmic_fading_speed = (-jnp.exp(incoming_entries[0])).reshape(
        attention_group_total, CHANNELS_PER_ATTN
    )
    extra_current_coeffs = incoming_entries[1].reshape(attention_group_total, CHANNELS_PER_ATTN)
    combined_attention_groups = (
        attention_mixing_complete(
            acceptance_entries,
            lookup_sources,
            payload_entries,
            1.0 - handed_onward,
            logarithmic_fading_speed,
            extra_current_coeffs,
        )
        / head_divisor
    )
    center = jnp.mean(combined_attention_groups, axis=2, keepdims=True)
    spread = jnp.mean(jnp.square(combined_attention_groups - center), axis=2, keepdims=True)
    grouped = ((combined_attention_groups - center) * lax.rsqrt(spread + group_eps)).reshape(
        token_count, unit_width
    )
    return (grouped * incoming_entries[2] + incoming_entries[3]) * jax.nn.silu(gate_pre)


def project_forward(stack_in, weights):
    gathered = lax.all_gather(stack_in, "row", axis=2, tiled=True)
    partials = [
        jnp.einsum(
            "tk,cwk->tcw", gathered[number], weights[number], preferred_element_type=jnp.float32
        )
        for number in range(len(weights))
    ]
    joined = jnp.concatenate(partials, axis=2)
    summed = lax.psum_scatter(joined, "col", scatter_dimension=1, tiled=True)
    return (gathered, summed[:, 0, :])


def project_backward(grad_out, gathered, weights):
    spread_out = lax.all_gather(grad_out[:, None, :], "col", axis=1, tiled=True)
    offset = 0
    grads_w = []
    grads_in = []
    for number in range(len(weights)):
        columns = weights[number].shape[1]
        block_grad = spread_out[:, :, offset : offset + columns]
        grads_w.append(
            jnp.einsum(
                "tk,tcw->cwk", gathered[number], block_grad, preferred_element_type=jnp.float32
            )
        )
        grads_in.append(
            jnp.einsum(
                "tcw,cwk->tk", block_grad, weights[number], preferred_element_type=jnp.float32
            )
        )
        offset = offset + columns
    summed = lax.psum_scatter(
        jnp.stack(grads_in).astype(jnp.bfloat16), "row", scatter_dimension=2, tiled=True
    ).astype(jnp.float32)
    return (summed, grads_w)


def run_forward(tokens_f, parameter_catalog, weights, handed_onward):
    w_recept, w_key, w_value, w_gate, w_output, ffn_key, ffn_value, ffn_recept = weights
    normed_one, unit_one, inverse_one = norm_forward(
        tokens_f, parameter_catalog[0], parameter_catalog[1]
    )
    mixes_one = mix_inputs(normed_one, parameter_catalog[2:6], handed_onward).astype(jnp.bfloat16)
    gathered_one, projected = project_forward(mixes_one, (w_recept, w_key, w_value, w_gate))
    gated_out = time_block(projected, parameter_catalog[6:10], handed_onward).astype(jnp.bfloat16)
    gathered_gated, branch = project_forward(gated_out[None], (w_output,))
    residual = tokens_f + branch
    normed_two, unit_two, inverse_two = norm_forward(
        residual, parameter_catalog[10], parameter_catalog[11]
    )
    mixes_two = mix_inputs(normed_two, parameter_catalog[12:14], handed_onward).astype(jnp.bfloat16)
    gathered_two, key_recept = project_forward(mixes_two, (ffn_key, ffn_recept))
    hidden_width = ffn_key.shape[1]
    hidden_pre = key_recept[:, :hidden_width]
    recept_pre = key_recept[:, hidden_width:]
    activated = jnp.square(jax.nn.relu(hidden_pre)).astype(jnp.bfloat16)
    gathered_act, payload_mapped = project_forward(activated[None], (ffn_value,))
    output = residual + jax.nn.sigmoid(recept_pre) * payload_mapped
    kept_state = (
        normed_one,
        unit_one,
        inverse_one,
        gathered_one,
        projected,
        gathered_gated,
        normed_two,
        unit_two,
        inverse_two,
        gathered_two,
        hidden_pre,
        recept_pre,
        gathered_act,
        payload_mapped,
    )
    return (output, kept_state)


def shards(
    tokens,
    segments,
    channel_table,
    w_recept,
    w_key,
    w_value,
    w_gate,
    w_output,
    ffn_key,
    ffn_value,
    ffn_recept,
    cotangent,
):
    tokens_f = tokens.astype(jnp.float32).T
    upstream = cotangent.astype(jnp.float32).T
    positions = jnp.arange(tokens_f.shape[0], dtype=jnp.int32)
    earlier = jnp.concatenate([segments[:1], segments[:-1]])
    handed_onward = 1.0 - ((positions % SEQ == 0) | (segments != earlier)).astype(jnp.float32)
    parameter_catalog = channel_table.astype(jnp.float32)
    weights = (w_recept, w_key, w_value, w_gate, w_output, ffn_key, ffn_value, ffn_recept)
    output, unused = run_forward(tokens_f, parameter_catalog, weights, handed_onward)
    tokens_again, upstream, output = lax.optimization_barrier((tokens_f, upstream, output))
    unused_out, kept_state = run_forward(tokens_again, parameter_catalog, weights, handed_onward)
    (
        normed_one,
        unit_one,
        inverse_one,
        gathered_one,
        projected,
        gathered_gated,
        normed_two,
        unit_two,
        inverse_two,
        gathered_two,
        hidden_pre,
        recept_pre,
        gathered_act,
        payload_mapped,
    ) = kept_state
    gate_value = jax.nn.sigmoid(recept_pre)
    grad_valued = (upstream * gate_value).astype(jnp.bfloat16)
    grad_recept = upstream * payload_mapped * gate_value * (1.0 - gate_value)
    grad_act, grads_value = project_backward(grad_valued, gathered_act, (ffn_value,))
    grad_hidden = grad_act[0] * 2.0 * jax.nn.relu(hidden_pre)
    grad_key_recept = jnp.concatenate([grad_hidden, grad_recept], axis=1).astype(jnp.bfloat16)
    grad_mixes_two, grads_ffn = project_backward(
        grad_key_recept, gathered_two, (ffn_key, ffn_recept)
    )
    unused_two, second_pull = jax.vjp(
        lambda normed, coeffs: mix_inputs(normed, coeffs, handed_onward),
        normed_two,
        parameter_catalog[12:14],
    )
    grad_normed_two, grad_coeff_two = second_pull(grad_mixes_two)
    grad_res_norm, gain_two, bias_two = norm_backward(
        grad_normed_two, unit_two, inverse_two, parameter_catalog[10]
    )
    grad_residual = upstream + grad_res_norm
    grad_gated, grads_output = project_backward(
        grad_residual.astype(jnp.bfloat16), gathered_gated, (w_output,)
    )
    unused_block, block_pull = jax.vjp(
        lambda projected_in, incoming_entries: time_block(
            projected_in, incoming_entries, handed_onward
        ),
        projected,
        parameter_catalog[6:10],
    )
    grad_projected, grad_rows = block_pull(grad_gated[0])
    grad_mixes_one, grads_time = project_backward(
        grad_projected.astype(jnp.bfloat16), gathered_one, (w_recept, w_key, w_value, w_gate)
    )
    unused_one, first_pull = jax.vjp(
        lambda normed, coeffs: mix_inputs(normed, coeffs, handed_onward),
        normed_one,
        parameter_catalog[2:6],
    )
    grad_normed_one, grad_coeff_one = first_pull(grad_mixes_one)
    grad_tok_norm, gain_one, bias_one = norm_backward(
        grad_normed_one, unit_one, inverse_one, parameter_catalog[0]
    )
    grad_tokens = grad_residual + grad_tok_norm
    table_grad = jnp.concatenate(
        [
            gain_one[None],
            bias_one[None],
            grad_coeff_one,
            grad_rows,
            gain_two[None],
            bias_two[None],
            grad_coeff_two,
        ],
        axis=0,
    )
    summed = (
        lax.psum(grads_time[0].astype(jnp.bfloat16), "dp").astype(jnp.float32),
        lax.psum(grads_time[1].astype(jnp.bfloat16), "dp").astype(jnp.float32),
        lax.psum(grads_time[2].astype(jnp.bfloat16), "dp").astype(jnp.float32),
        lax.psum(grads_time[3].astype(jnp.bfloat16), "dp").astype(jnp.float32),
        lax.psum(grads_output[0].astype(jnp.bfloat16), "dp").astype(jnp.float32),
        lax.psum(grads_ffn[0].astype(jnp.bfloat16), "dp").astype(jnp.float32),
        lax.psum(grads_value[0].astype(jnp.bfloat16), "dp").astype(jnp.float32),
        lax.psum(grads_ffn[1].astype(jnp.bfloat16), "dp").astype(jnp.float32),
        lax.psum(table_grad.astype(jnp.bfloat16), "dp").astype(jnp.float32),
    )
    return (
        output.astype(jnp.bfloat16).T,
        grad_tokens.T,
        summed[8],
        summed[0],
        summed[1],
        summed[2],
        summed[3],
        summed[4],
        summed[5],
        summed[6],
        summed[7],
    )


def solution(mesh):
    in_specs = (
        P(("col", "row"), "dp"),
        P("dp"),
        P(None, ("col", "row")),
        P(None, "row", "col"),
        P(None, "row", "col"),
        P(None, "row", "col"),
        P(None, "row", "col"),
        P(None, "row", "col"),
        P(None, "row", "col"),
        P(None, "row", "col"),
        P(None, "row", "col"),
        P(("col", "row"), "dp"),
    )
    out_specs = (
        P(("col", "row"), "dp"),
        P(("col", "row"), "dp"),
        P(None, ("col", "row")),
        P(None, "row", "col"),
        P(None, "row", "col"),
        P(None, "row", "col"),
        P(None, "row", "col"),
        P(None, "row", "col"),
        P(None, "row", "col"),
        P(None, "row", "col"),
        P(None, "row", "col"),
    )
    return jax.shard_map(shards, mesh=mesh, in_specs=in_specs, out_specs=out_specs, check_vma=False)
```

profile of v0, /device:TPU:0, one launch (start us, length us, event | category | flops | bytes accessed | tf_op | source)
XLA Modules:
  0.0 4988.6 jit_solution(13791718364554033619)
XLA Ops:
  12.2 36.0 psum.133
  90.2 58.4 %all-gather.20.cloned.1.call-done = bf16[4,2048,512]{2,1,0:T(8,128)(2,1)} async-done(((bf16[4,2048,128]{2,1,0:T(8,128)(2,1)}), bf16[4,2048,512]{2,1,0:T(8,128)(2,1)}) %all-gather.20.cloned.1.call-update) | async-done | bytes 8388624 | tf_op jit(solution)/shard_map/all_gather | solution.py:169
  165.3 278.8 %reduce-scatter.17.cloned.1.call-done = f32[2048,1,512]{0,2,1:T(8,128)} async-done(((f32[2048,4,512]{0,2,1:T(8,128)}), f32[2048,1,512]{0,2,1:T(8,128)}) %reduce-scatter.17.cloned.1.call-update) | async-done | bytes 4194320 | tf_op jit(solution)/shard_map/reduce_scatter | solution.py:177
  457.3 281.5 %while.72 = (s32[]{:T(128)}, f32[2,64,64]{2,1,0:T(8,128)S(1)}, f32[32,64,2,64]{3,1,2,0:T(8,128)}, f32[2,64]{1,0:T(2,128)S(1)}, f32[32,64]{1,0:T(8,128)S(1)}, /*i...) while((s32[]{:T(128)}, f32[2,64,64]{2,1,0:T(8,128)S(1)}, ...), condition=%wide.region_8.9_spmd.clone, body=%wide.region_5.8_spmd.clone.sunk | while | flops 25355200 | bytes 1069532 | solution.py:120
  782.2 76.1 %reduce-scatter.19.cloned.1.call-done = f32[2048,1,128]{0,2,1:T(8,128)} async-done(((f32[2048,4,128]{0,2,1:T(8,128)}), f32[2048,1,128]{0,2,1:T(8,128)}) %reduce-scatter.19.cloned.1.call-update) | async-done | bytes 1048592 | tf_op jit(solution)/shard_map/reduce_scatter | solution.py:177
  859.8 33.6 psum.135
  934.9 33.7 all-gather.22.cloned.1.call-done
  983.0 313.9 %reduce-scatter.21.cloned.1.call-done = f32[2048,1,576]{0,2,1:T(8,128)} async-done(((f32[2048,4,576]{0,2,1:T(8,128)}), f32[2048,1,576]{0,2,1:T(8,128)}) %reduce-scatter.21.cloned.1.call-update) | async-done | bytes 4718608 | tf_op jit(solution)/shard_map/reduce_scatter | solution.py:177
  1300.7 53.5 %all-gather.32.cloned.1.call-done = bf16[2048,1792]{0,1:T(8,128)(2,1)} async-done(((bf16[2048,448]{0,1:T(8,128)(2,1)}), bf16[2048,1792]{0,1:T(8,128)(2,1)}) %all-gather.32.cloned.1.call-update) | async-done | bytes 7340048 | tf_op jit(solution)/shard_map/all_gather | solution.py:169
  1366.5 74.2 %reduce-scatter.23.cloned.1.call-done = f32[2048,1,128]{0,2,1:T(8,128)} async-done(((f32[2048,4,128]{0,2,1:T(8,128)}), f32[2048,1,128]{0,2,1:T(8,128)}) %reduce-scatter.23.cloned.1.call-update) | async-done | bytes 1048592 | tf_op jit(solution)/shard_map/reduce_scatter | solution.py:177
  1443.8 33.6 psum.137
  1520.4 58.6 %all-gather.24.cloned.1.call-done = bf16[4,2048,512]{2,1,0:T(8,128)(2,1)} async-done(((bf16[4,2048,128]{2,1,0:T(8,128)(2,1)}), bf16[4,2048,512]{2,1,0:T(8,128)(2,1)}) %all-gather.24.cloned.1.call-update) | async-done | bytes 8388624 | tf_op jit(solution)/shard_map/all_gather | solution.py:169
  1594.7 279.7 %reduce-scatter.25.cloned.1.call-done = f32[2048,1,512]{0,2,1:T(8,128)} async-done(((f32[2048,4,512]{0,2,1:T(8,128)}), f32[2048,1,512]{0,2,1:T(8,128)}) %reduce-scatter.25.cloned.1.call-update) | async-done | bytes 4194320 | tf_op jit(solution)/shard_map/reduce_scatter | solution.py:177
  1898.1 355.7 %while.73 = (s32[]{:T(128)}, f32[2,64,64]{2,1,0:T(8,128)S(1)}, f32[32,64,2,64]{3,1,2,0:T(8,128)}, f32[2,64]{1,0:T(2,128)S(1)}, f32[32,64]{1,0:T(8,128)}, /*index...) while((s32[]{:T(128)}, f32[2,64,64]{2,1,0:T(8,128)S(1)}, ...), condition=%wide.region_26.27_spmd.clone, body=%wide.region_23.26_spmd.clone.sunk | while | flops 25355200 | bytes 975315 | solution.py:120
  2255.4 331.4 %while.75 = (s32[]{:T(128)}, f32[2,64,64]{2,1,0:T(8,128)S(1)}, f32[32,64,2,64]{3,1,2,0:T(8,128)}, f32[32,2,64,64]{3,2,1,0:T(8,128)}, f32[2,64,1]{1,0,2:T(2,128)S...) while((s32[]{:T(128)}, f32[2,64,64]{2,1,0:T(8,128)S(1)}, ...), condition=%wide.region_46.47_spmd.clone.clone.clone.clone, body=%wide.region_43.46_spmd.clone.clone.clone.clone.sunk | while | flops 25362944 | bytes 1068772 | solution.py:120
  2631.7 76.9 %reduce-scatter.27.cloned.1.call-done = f32[2048,1,128]{0,2,1:T(8,128)} async-done(((f32[2048,4,128]{0,2,1:T(8,128)}), f32[2048,1,128]{0,2,1:T(8,128)}) %reduce-scatter.27.cloned.1.call-update) | async-done | bytes 1048592 | tf_op jit(solution)/shard_map/reduce_scatter | solution.py:177
  2710.9 34.0 psum.139
  2786.1 34.1 all-gather.26.cloned.1.call-done
  2834.6 313.9 %reduce-scatter.29.cloned.1.call-done = f32[2048,1,576]{0,2,1:T(8,128)} async-done(((f32[2048,4,576]{0,2,1:T(8,128)}), f32[2048,1,576]{0,2,1:T(8,128)}) %reduce-scatter.29.cloned.1.call-update) | async-done | bytes 4718608 | tf_op jit(solution)/shard_map/reduce_scatter | solution.py:177
  3152.2 53.5 %all-gather.38.cloned.1.call-done = bf16[2048,1792]{0,1:T(8,128)(2,1)} async-done(((bf16[2048,448]{0,1:T(8,128)(2,1)}), bf16[2048,1792]{0,1:T(8,128)(2,1)}) %all-gather.38.cloned.1.call-update) | async-done | bytes 7340048 | tf_op jit(solution)/shard_map/all_gather | solution.py:169
  3215.3 76.9 %reduce-scatter.33.cloned.1.call-done = f32[2048,1,128]{0,2,1:T(8,128)} async-done(((f32[2048,4,128]{0,2,1:T(8,128)}), f32[2048,1,128]{0,2,1:T(8,128)}) %reduce-scatter.33.cloned.1.call-update) | async-done | bytes 1048592 | tf_op jit(solution)/shard_map/reduce_scatter | solution.py:177
  3295.2 46.4 all-gather.36.cloned.1.call-done
  3350.8 64.3 %reduce-scatter.31.cloned.1.call-done = bf16[1,2048,448]{1,2,0:T(8,128)(2,1)} async-done(((bf16[1,2048,1792]{1,2,0:T(8,128)(2,1)}), bf16[1,2048,448]{1,2,0:T(8,128)(2,1)}) %reduce-scatter.31.cloned.1.call-update) | async-done | bytes 1835024 | tf_op jit(solution)/shard_map/reduce_scatter | solution.py:200
  3420.1 166.9 %all-gather.28.cloned.1.call-done = bf16[2048,4,576]{0,2,1:T(8,128)(2,1)} async-done(((bf16[2048,1,576]{0,2,1:T(8,128)(2,1)}), bf16[2048,4,576]{0,2,1:T(8,128)(2,1)}) %all-gather.28.cloned.1.call-update) | async-done | bytes 9437200 | tf_op jit(solution)/shard_map/all_gather | solution.py:182
  3616.1 42.7 reduce-scatter.37.cloned.1.call-done
  3678.0 60.7 %psum.141 = f32[2,2048]{1,0:T(2,128)S(1)} all-reduce(f32[2,2048]{1,0:T(2,128)S(1)} %pad_maximum_fusion.7), channel_id=1, replica_groups=mesh['dp'=2,'row'=4,'col'=4] {'row','col'}, use_global_device_ids=true, to_apply=%region_42.43 | all-reduce | flops 4096 | bytes 32768 | tf_op jit(solution)/shard_map/psum | solution.py:17
  3741.5 44.3 all-gather.40.cloned.1.call-done
  3842.9 629.8 %while.74 = (s32[]{:T(128)}, f32[2,64]{1,0:T(2,128)S(1)}, f32[2,64]{1,0:T(2,128)S(1)}, f32[2,64,64]{2,1,0:T(8,128)S(1)}, f32[32,64,2,64]{1,0,3,2:T(8,128)}, /*in...) while((s32[]{:T(128)}, f32[2,64]{1,0:T(2,128)S(1)}, ...), condition=%wide.region_62.63_spmd.clone, body=%wide.region_53.62_spmd.clone.sunk | while | flops 57132356 | bytes 2100241 | solution.py:120
  4508.6 126.1 %all-gather.42.cloned.1.call-done = bf16[2048,2048]{0,1:T(8,128)(2,1)} async-done(((bf16[2048,512]{0,1:T(8,128)(2,1)}), bf16[2048,2048]{0,1:T(8,128)(2,1)}) %all-gather.42.cloned.1.call-update) | async-done | bytes 8388624 | tf_op jit(solution)/shard_map/all_gather | solution.py:182
  4697.2 119.0 %all-reduce.17.cloned.1.call-done = (bf16[4,128,512]{2,1,0:T(8,128)(2,1)}, bf16[4,128,512]{2,1,0:T(8,128)(2,1)}, bf16[4,128,512]{2,1,0:T(8,128)(2,1)}, bf16[4,12...) async-done(((bf16[4,128,512]{2,1,0:T(8,128)(2,1)}, ...) | async-done | bytes 6815760 | tf_op jit(solution)/shard_map/psum | solution.py:342
  4829.9 60.6 %reduce-scatter.39.cloned.1.call-done = bf16[128,8192]{1,0:T(8,128)(2,1)} async-done(((bf16[512,8192]{1,0:T(8,128)(2,1)}), bf16[128,8192]{1,0:T(8,128)(2,1)}) %reduce-scatter.39.cloned.1.call-update) | async-done | bytes 2097168
  4912.4 60.7 %psum.142 = f32[2,2048]{1,0:T(2,128)S(1)} all-reduce(f32[2,2048]{1,0:T(2,128)S(1)} %pad_maximum_fusion.8), channel_id=1, replica_groups=mesh['dp'=2,'row'=4,'col'=4] {'row','col'}, use_global_device_ids=true, to_apply=%region_68.69 | all-reduce | flops 4096 | bytes 32768 | tf_op jit(solution)/shard_map/psum | solution.py:17
  (3664 shorter events, 2249.7 us)
Async XLA Ops:
  7.2 964.5 %copy-start = (bf16[4,448,512]{2,1,0:T(8,128)(2,1)S(1)}, bf16[4,448,512]{2,1,0:T(8,128)(2,1)}, u32[]{:S(2)}) copy-start(bf16[4,448,512]{2,1,0:T(8,128)(2,1)} %param.28) | copy-start | bytes 5505028
  7.2 141.4 %all-gather.20.cloned.1.call-start = ((), (), s32[]{:S(2)}) async-start(), calls=%async_computation.12 | async-start | bytes 10485760 | tf_op jit(solution)/shard_map/all_gather | solution.py:169
  8.1 774.2 %copy-start.41 = (f32[14,128]{1,0:T(8,128)}, f32[14,128]{1,0:T(8,128)S(1)}, u32[]{:S(2)}) copy-start(f32[14,128]{1,0:T(8,128)S(1)} %convert_element_type.306) | copy-start | bytes 21508
  9.1 915.0 %copy-start.45 = (f32[128]{0:T(128)}, f32[128]{0:T(128)S(1)}, u32[]{:S(2)}) copy-start(f32[128]{0:T(128)S(1)} %get-tuple-element.1371) | copy-start | bytes 1540
  9.1 1499.0 %copy-start.43 = (f32[128]{0:T(128)}, f32[128]{0:T(128)S(1)}, u32[]{:S(2)}) copy-start(f32[128]{0:T(128)S(1)} %get-tuple-element.1369) | copy-start | bytes 1540
  9.1 1507.8 %copy-start.36 = (f32[4,128]{1,0:T(4,128)}, f32[4,128]{1,0:T(4,128)S(1)}, u32[]{:S(2)}) copy-start(f32[4,128]{1,0:T(4,128)S(1)} %broadcast_subtract_fusion.4) | copy-start | bytes 6148
  9.8 1507.1 %copy-start.38 = (f32[4,128]{1,0:T(4,128)}, f32[4,128]{1,0:T(4,128)S(1)}, u32[]{:S(2)}) copy-start(f32[4,128]{1,0:T(4,128)S(1)} %slice.306) | copy-start | bytes 6148
  90.2 353.9 %reduce-scatter.17.cloned.1.call-start = ((), (), s32[]{:S(2)}) async-start(), calls=%async_computation.13 | async-start | bytes 20971520 | tf_op jit(solution)/shard_map/reduce_scatter | solution.py:177
  163.7 613.0 %all-gather.30.cloned.1.call-start = ((), (), s32[]{:S(2)}) async-start(), calls=%async_computation.27 | async-start | bytes 2621440 | tf_op jit(solution)/shard_map/all_gather | solution.py:169
  753.2 105.2 %reduce-scatter.19.cloned.1.call-start = ((), (), s32[]{:S(2)}) async-start(), calls=%async_computation.14 | async-start | bytes 5242880 | tf_op jit(solution)/shard_map/reduce_scatter | solution.py:177
  781.4 187.2 %all-gather.22.cloned.1.call-start = ((), (), s32[]{:S(2)}) async-start(), calls=%async_computation.15 | async-start | bytes 5242880 | tf_op jit(solution)/shard_map/all_gather | solution.py:169
  934.4 362.5 %reduce-scatter.21.cloned.1.call-start = ((), (), s32[]{:S(2)}) async-start(), calls=%async_computation.16 | async-start | bytes 23592960 | tf_op jit(solution)/shard_map/reduce_scatter | solution.py:177
  983.0 371.2 %all-gather.32.cloned.1.call-start = ((), (), s32[]{:S(2)}) async-start(), calls=%async_computation.28 | async-start | bytes 9175040 | tf_op jit(solution)/shard_map/all_gather | solution.py:169
  1300.6 140.1 %reduce-scatter.23.cloned.1.call-start = ((), (), s32[]{:S(2)}) async-start(), calls=%async_computation.17 | async-start | bytes 5242880 | tf_op jit(solution)/shard_map/reduce_scatter | solution.py:177
  1363.9 215.1 %all-gather.24.cloned.1.call-start = ((), (), s32[]{:S(2)}) async-start(), calls=%async_computation.18 | async-start | bytes 10485760 | tf_op jit(solution)/shard_map/all_gather | solution.py:169
  1364.0 1344.5 %copy-start.2 = (f32[2048,128]{0,1:T(8,128)}, f32[2048,128]{0,1:T(8,128)S(1)}, u32[]{:S(2)}) copy-start(f32[2048,128]{0,1:T(8,128)S(1)} %convert_bitcast_fusion) | copy-start | bytes 3145732
  1520.4 354.1 %reduce-scatter.25.cloned.1.call-start = ((), (), s32[]{:S(2)}) async-start(), calls=%async_computation.19 | async-start | bytes 20971520 | tf_op jit(solution)/shard_map/reduce_scatter | solution.py:177
  1594.0 1032.7 %all-gather.34.cloned.1.call-start = ((), (), s32[]{:S(2)}) async-start(), calls=%async_computation.29 | async-start | bytes 2621440 | tf_op jit(solution)/shard_map/all_gather | solution.py:169
  2603.2 105.3 %reduce-scatter.27.cloned.1.call-start = ((), (), s32[]{:S(2)}) async-start(), calls=%async_computation.20 | async-start | bytes 5242880 | tf_op jit(solution)/shard_map/reduce_scatter | solution.py:177
  2631.7 188.6 %all-gather.26.cloned.1.call-start = ((), (), s32[]{:S(2)}) async-start(), calls=%async_computation.21 | async-start | bytes 5242880 | tf_op jit(solution)/shard_map/all_gather | solution.py:169
  2786.1 362.4 %reduce-scatter.29.cloned.1.call-start = ((), (), s32[]{:S(2)}) async-start(), calls=%async_computation.22 | async-start | bytes 23592960 | tf_op jit(solution)/shard_map/reduce_scatter | solution.py:177
  2834.5 371.2 %all-gather.38.cloned.1.call-start = ((), (), s32[]{:S(2)}) async-start(), calls=%async_computation.31 | async-start | bytes 9175040 | tf_op jit(solution)/shard_map/all_gather | solution.py:169
  3152.2 140.0 %reduce-scatter.33.cloned.1.call-start = ((), (), s32[]{:S(2)}) async-start(), calls=%async_computation.24 | async-start | bytes 5242880 | tf_op jit(solution)/shard_map/reduce_scatter | solution.py:177
  3215.3 126.3 %all-gather.36.cloned.1.call-start = ((), (), s32[]{:S(2)}) async-start(), calls=%async_computation.30 | async-start | bytes 2621440 | tf_op jit(solution)/shard_map/all_gather | solution.py:182
  3295.0 120.1 %reduce-scatter.31.cloned.1.call-start = ((), (), s32[]{:S(2)}) async-start(), calls=%async_computation.23 | async-start | bytes 9175040 | tf_op jit(solution)/shard_map/reduce_scatter | solution.py:200
  3350.7 236.3 %all-gather.28.cloned.1.call-start = ((), (), s32[]{:S(2)}) async-start(), calls=%async_computation.25 | async-start | bytes 11796480 | tf_op jit(solution)/shard_map/all_gather | solution.py:182
  3420.0 238.7 %reduce-scatter.37.cloned.1.call-start = ((), (), s32[]{:S(2)}) async-start(), calls=%async_computation.34 | async-start | bytes 5242880
  3615.9 169.9 %all-gather.40.cloned.1.call-start = ((), (), s32[]{:S(2)}) async-start(), calls=%async_computation.32 | async-start | bytes 2621440 | tf_op jit(solution)/shard_map/all_gather | solution.py:182
  3741.5 78.9 %reduce-scatter.35.cloned.1.call-start = ((), (), s32[]{:S(2)}) async-start(), calls=%async_computation.26 | async-start | bytes 2621440 | tf_op jit(solution)/shard_map/reduce_scatter | solution.py:200
  3790.1 844.6 %all-gather.42.cloned.1.call-start = ((), (), s32[]{:S(2)}) async-start(), calls=%async_computation.33 | async-start | bytes 10485760 | tf_op jit(solution)/shard_map/all_gather | solution.py:182
  4484.9 331.3 %all-reduce.17.cloned.1.call-start = ((), (), s32[]{:S(2)}) async-start(), calls=%async_computation.36 | async-start | bytes 13631488 | tf_op jit(solution)/shard_map/psum | solution.py:342
  4650.9 239.7 %reduce-scatter.39.cloned.1.call-start = ((), (), s32[]{:S(2)}) async-start(), calls=%async_computation.35 | async-start | bytes 10485760
  (71 other events, 1018.4 us)
Sparse Core Ops, SparseCore 0:
  90.3 58.2 all-gather.19
  163.8 280.2 reduce-scatter.16
  753.3 23.2 all-gather.29
  781.6 76.7 reduce-scatter.18
  934.5 33.9 all-gather.21
  983.1 313.7 reduce-scatter.20
  1300.8 53.3 all-gather.31
  1364.0 76.7 reduce-scatter.22
  1520.5 58.4 all-gather.23
  1594.1 280.2 reduce-scatter.24
  2603.3 23.3 all-gather.33
  2631.8 76.7 reduce-scatter.26
  2786.2 33.9 all-gather.25
  2834.6 313.7 reduce-scatter.28
  3152.3 53.3 all-gather.37
  3215.4 76.7 reduce-scatter.32
  3295.1 46.4 all-gather.35
  3350.8 64.1 reduce-scatter.30
  3420.2 166.7 all-gather.27
  3616.1 42.6 reduce-scatter.36
  3741.6 44.1 all-gather.39
  3790.2 30.1 reduce-scatter.34
  4485.0 149.6 all-gather.41
  4651.0 165.1 all-reduce.16
  4818.8 71.7 reduce-scatter.38
where the time goes:
time: 5030 us; the launch traced here: 4990 us
  waiting for transfers between devices  2520 us (50%)
  local copies, waits for them, and re-layouts  886 us (18%)
  matrix products  629 us (13%)
  other arithmetic  539 us (11%)
  blocking collectives  385 us (8%)
    reduce_scatter x8, waiting for transfers between devices, project_forward(): summed = lax.psum_scatter(joined, 'col', scatter_dimension=1, tiled=True)  1490 us
    all_gather x4, waiting for transfers between devices, project_backward(): spread_out = lax.all_gather(grad_out[:, None, :], 'col', axis=1, tiled=True)  384 us
    psum x10, blocking collectives, feature_sums(): return lax.psum(stacked, ('row', 'col'))  380 us
    all_gather x8, waiting for transfers between devices, project_forward(): gathered = lax.all_gather(stack_in, 'row', axis=2, tiled=True)  339 us
    dynamic_update_slice x160, local copies, waits for them, and re-layouts, attention_mixing_complete(): lax.scan(step_fn, initial, (reshaped(acceptance_entries), reshaped(lookup...  282 us
    dot_general x160, matrix products, attention_mixing_segmented(): jnp.einsum('shi,shj->hij', end_k * tail_mask[:, None, None], payload_entr...  173 us
    dynamic_slice x256, local copies, waits for them, and re-layouts, attention_mixing_complete(): lax.scan(step_fn, initial, (reshaped(acceptance_entries), reshaped(lookup...  149 us
    mul x96, other arithmetic, attention_mixing_segmented(): jnp.sum(acceptance_entries * extra_current_coeffs[None] * lookup_sources,...  127 us
  transfers between devices with their start and end apart: 25, of which 25 were waited for; matrix products, arithmetic and copies ran while one was open for 2% of the time, Pallas kernels for 0%

commit v1 on v0

--- a/solution.py
+++ b/solution.py
@@ -14,7 +14,7 @@
 
 
 def feature_sums(stacked):
-    return lax.psum(stacked, ("row", "col"))
+    return jnp.sum(lax.all_gather(stacked, axis_name=("row", "col")), 0)
 
 
 def norm_forward(payload_entries, gain, bias):

time: 5030 us -> 4970 us (0.988)
  blocking collectives: 385 us -> 324 us
    psum x10 -> x0, blocking collectives: 380 us -> none  [feature_sums(): return lax.psum(stacked, ('row', 'col'))]
    all_gather x0 -> x10, blocking collectives: none -> 319 us  [feature_sums(): return jnp.sum(lax.all_gather(stacked, axis_name=('row', 'col')), 0)]
where the time goes in v1:
time: 4970 us; the launch traced here: 4930 us
  waiting for transfers between devices  2520 us (51%)
  local copies, waits for them, and re-layouts  891 us (18%)
  matrix products  629 us (13%)
  other arithmetic  543 us (11%)
  blocking collectives  324 us (7%)
    reduce_scatter x8, waiting for transfers between devices, project_forward(): summed = lax.psum_scatter(joined, 'col', scatter_dimension=1, tiled=True)  1490 us
    all_gather x4, waiting for transfers between devices, project_backward(): spread_out = lax.all_gather(grad_out[:, None, :], 'col', axis=1, tiled=True)  383 us
    all_gather x8, waiting for transfers between devices, project_forward(): gathered = lax.all_gather(stack_in, 'row', axis=2, tiled=True)  339 us
    all_gather x10, blocking collectives, feature_sums(): return jnp.sum(lax.all_gather(stacked, axis_name=('row', 'col')), 0)  319 us
    dynamic_update_slice x160, local copies, waits for them, and re-layouts, attention_mixing_complete(): lax.scan(step_fn, initial, (reshaped(acceptance_entries), reshaped(lookup...  282 us
    dot_general x160, matrix products, attention_mixing_segmented(): jnp.einsum('shi,shj->hij', end_k * tail_mask[:, None, None], payload_entr...  173 us
    dynamic_slice x256, local copies, waits for them, and re-layouts, attention_mixing_complete(): lax.scan(step_fn, initial, (reshaped(acceptance_entries), reshaped(lookup...  149 us
    mul x96, other arithmetic, attention_mixing_segmented(): jnp.sum(acceptance_entries * extra_current_coeffs[None] * lookup_sources,...  127 us
  transfers between devices with their start and end apart: 25, of which 25 were waited for; matrix products, arithmetic and copies ran while one was open for 2% of the time, Pallas kernels for 0%

profile of v1, /device:TPU:0, one launch (start us, length us, event | category | flops | bytes accessed | tf_op | source)
XLA Modules:
  0.0 4934.7 jit_solution(14432998060767174255)
XLA Ops:
  12.2 35.0 all-gather
  87.6 58.3 %all-gather.32.cloned.1.call-done = bf16[4,2048,512]{2,1,0:T(8,128)(2,1)} async-done(((bf16[4,2048,128]{2,1,0:T(8,128)(2,1)}), bf16[4,2048,512]{2,1,0:T(8,128)(2,1)}) %all-gather.32.cloned.1.call-update) | async-done | bytes 8388624 | tf_op jit(solution)/shard_map/all_gather | solution.py:169
  162.0 279.3 %reduce-scatter.17.cloned.1.call-done = f32[2048,1,512]{0,2,1:T(8,128)} async-done(((f32[2048,4,512]{0,2,1:T(8,128)}), f32[2048,1,512]{0,2,1:T(8,128)}) %reduce-scatter.17.cloned.1.call-update) | async-done | bytes 4194320 | tf_op jit(solution)/shard_map/reduce_scatter | solution.py:177
  455.5 281.5 %while.72 = (s32[]{:T(128)}, f32[2,64,64]{2,1,0:T(8,128)S(1)}, f32[32,64,2,64]{3,1,2,0:T(8,128)}, f32[2,64]{1,0:T(2,128)S(1)}, f32[32,64]{1,0:T(8,128)S(1)}, /*i...) while((s32[]{:T(128)}, f32[2,64,64]{2,1,0:T(8,128)S(1)}, ...), condition=%wide.region_8.9_spmd.clone, body=%wide.region_5.8_spmd.clone.sunk | while | flops 25355200 | bytes 1069532 | solution.py:120
  782.5 75.1 %reduce-scatter.19.cloned.1.call-done = f32[2048,1,128]{0,2,1:T(8,128)} async-done(((f32[2048,4,128]{0,2,1:T(8,128)}), f32[2048,1,128]{0,2,1:T(8,128)}) %reduce-scatter.19.cloned.1.call-update) | async-done | bytes 1048592 | tf_op jit(solution)/shard_map/reduce_scatter | solution.py:177
  859.1 32.6 all-gather.3
  936.8 33.7 all-gather.34.cloned.1.call-done
  984.9 313.9 %reduce-scatter.21.cloned.1.call-done = f32[2048,1,576]{0,2,1:T(8,128)} async-done(((f32[2048,4,576]{0,2,1:T(8,128)}), f32[2048,1,576]{0,2,1:T(8,128)}) %reduce-scatter.21.cloned.1.call-update) | async-done | bytes 4718608 | tf_op jit(solution)/shard_map/reduce_scatter | solution.py:177
  1302.6 53.5 %all-gather.44.cloned.1.call-done = bf16[2048,1792]{0,1:T(8,128)(2,1)} async-done(((bf16[2048,448]{0,1:T(8,128)(2,1)}), bf16[2048,1792]{0,1:T(8,128)(2,1)}) %all-gather.44.cloned.1.call-update) | async-done | bytes 7340048 | tf_op jit(solution)/shard_map/all_gather | solution.py:169
  1368.4 74.2 %reduce-scatter.23.cloned.1.call-done = f32[2048,1,128]{0,2,1:T(8,128)} async-done(((f32[2048,4,128]{0,2,1:T(8,128)}), f32[2048,1,128]{0,2,1:T(8,128)}) %reduce-scatter.23.cloned.1.call-update) | async-done | bytes 1048592 | tf_op jit(solution)/shard_map/reduce_scatter | solution.py:177
  1445.7 32.6 all-gather.6
  1520.6 58.6 %all-gather.36.cloned.1.call-done = bf16[4,2048,512]{2,1,0:T(8,128)(2,1)} async-done(((bf16[4,2048,128]{2,1,0:T(8,128)(2,1)}), bf16[4,2048,512]{2,1,0:T(8,128)(2,1)}) %all-gather.36.cloned.1.call-update) | async-done | bytes 8388624 | tf_op jit(solution)/shard_map/all_gather | solution.py:169
  1594.9 279.7 %reduce-scatter.25.cloned.1.call-done = f32[2048,1,512]{0,2,1:T(8,128)} async-done(((f32[2048,4,512]{0,2,1:T(8,128)}), f32[2048,1,512]{0,2,1:T(8,128)}) %reduce-scatter.25.cloned.1.call-update) | async-done | bytes 4194320 | tf_op jit(solution)/shard_map/reduce_scatter | solution.py:177
  1898.2 355.7 %while.73 = (s32[]{:T(128)}, f32[2,64,64]{2,1,0:T(8,128)S(1)}, f32[32,64,2,64]{3,1,2,0:T(8,128)}, f32[2,64]{1,0:T(2,128)S(1)}, f32[32,64]{1,0:T(8,128)}, /*index...) while((s32[]{:T(128)}, f32[2,64,64]{2,1,0:T(8,128)S(1)}, ...), condition=%wide.region_26.27_spmd.clone, body=%wide.region_23.26_spmd.clone.sunk | while | flops 25355200 | bytes 975315 | solution.py:120
  2255.6 331.4 %while.75 = (s32[]{:T(128)}, f32[2,64,64]{2,1,0:T(8,128)S(1)}, f32[32,64,2,64]{3,1,2,0:T(8,128)}, f32[32,2,64,64]{3,2,1,0:T(8,128)}, f32[2,64,1]{1,0,2:T(2,128)S...) while((s32[]{:T(128)}, f32[2,64,64]{2,1,0:T(8,128)S(1)}, ...), condition=%wide.region_46.47_spmd.clone.clone.clone.clone, body=%wide.region_43.46_spmd.clone.clone.clone.clone.sunk | while | flops 25362944 | bytes 1068772 | solution.py:120
  2631.9 76.8 %reduce-scatter.27.cloned.1.call-done = f32[2048,1,128]{0,2,1:T(8,128)} async-done(((f32[2048,4,128]{0,2,1:T(8,128)}), f32[2048,1,128]{0,2,1:T(8,128)}) %reduce-scatter.27.cloned.1.call-update) | async-done | bytes 1048592 | tf_op jit(solution)/shard_map/reduce_scatter | solution.py:177
  2711.1 33.2 all-gather.9
  2787.1 34.1 all-gather.38.cloned.1.call-done
  2835.6 313.9 %reduce-scatter.29.cloned.1.call-done = f32[2048,1,576]{0,2,1:T(8,128)} async-done(((f32[2048,4,576]{0,2,1:T(8,128)}), f32[2048,1,576]{0,2,1:T(8,128)}) %reduce-scatter.29.cloned.1.call-update) | async-done | bytes 4718608 | tf_op jit(solution)/shard_map/reduce_scatter | solution.py:177
  3153.3 53.5 %all-gather.50.cloned.1.call-done = bf16[2048,1792]{0,1:T(8,128)(2,1)} async-done(((bf16[2048,448]{0,1:T(8,128)(2,1)}), bf16[2048,1792]{0,1:T(8,128)(2,1)}) %all-gather.50.cloned.1.call-update) | async-done | bytes 7340048 | tf_op jit(solution)/shard_map/all_gather | solution.py:169
  3216.3 76.9 %reduce-scatter.33.cloned.1.call-done = f32[2048,1,128]{0,2,1:T(8,128)} async-done(((f32[2048,4,128]{0,2,1:T(8,128)}), f32[2048,1,128]{0,2,1:T(8,128)}) %reduce-scatter.33.cloned.1.call-update) | async-done | bytes 1048592 | tf_op jit(solution)/shard_map/reduce_scatter | solution.py:177
  3296.5 46.4 all-gather.48.cloned.1.call-done
  3352.1 64.3 %reduce-scatter.31.cloned.1.call-done = bf16[1,2048,448]{1,2,0:T(8,128)(2,1)} async-done(((bf16[1,2048,1792]{1,2,0:T(8,128)(2,1)}), bf16[1,2048,448]{1,2,0:T(8,128)(2,1)}) %reduce-scatter.31.cloned.1.call-update) | async-done | bytes 1835024 | tf_op jit(solution)/shard_map/reduce_scatter | solution.py:200
  3421.4 166.9 %all-gather.40.cloned.1.call-done = bf16[2048,4,576]{0,2,1:T(8,128)(2,1)} async-done(((bf16[2048,1,576]{0,2,1:T(8,128)(2,1)}), bf16[2048,4,576]{0,2,1:T(8,128)(2,1)}) %all-gather.40.cloned.1.call-update) | async-done | bytes 9437200 | tf_op jit(solution)/shard_map/all_gather | solution.py:182
  3617.4 42.7 reduce-scatter.37.cloned.1.call-done
  3678.2 33.7 all-gather.17
  3714.9 43.8 all-gather.52.cloned.1.call-done
  3815.8 629.8 %while.74 = (s32[]{:T(128)}, f32[2,64]{1,0:T(2,128)S(1)}, f32[2,64]{1,0:T(2,128)S(1)}, f32[2,64,64]{2,1,0:T(8,128)S(1)}, f32[32,64,2,64]{1,0,3,2:T(8,128)}, /*in...) while((s32[]{:T(128)}, f32[2,64]{1,0:T(2,128)S(1)}, ...), condition=%wide.region_62.63_spmd.clone, body=%wide.region_53.62_spmd.clone.sunk | while | flops 57132356 | bytes 2100241 | solution.py:120
  4481.5 126.2 %all-gather.54.cloned.1.call-done = bf16[2048,2048]{0,1:T(8,128)(2,1)} async-done(((bf16[2048,512]{0,1:T(8,128)(2,1)}), bf16[2048,2048]{0,1:T(8,128)(2,1)}) %all-gather.54.cloned.1.call-update) | async-done | bytes 8388624 | tf_op jit(solution)/shard_map/all_gather | solution.py:182
  4670.1 119.0 %all-reduce.17.cloned.1.call-done = (bf16[4,128,512]{2,1,0:T(8,128)(2,1)}, bf16[4,128,512]{2,1,0:T(8,128)(2,1)}, bf16[4,128,512]{2,1,0:T(8,128)(2,1)}, bf16[4,12...) async-done(((bf16[4,128,512]{2,1,0:T(8,128)(2,1)}, ...) | async-done | bytes 6815760 | tf_op jit(solution)/shard_map/psum | solution.py:342
  4802.8 60.6 %reduce-scatter.39.cloned.1.call-done = bf16[128,8192]{1,0:T(8,128)(2,1)} async-done(((bf16[512,8192]{1,0:T(8,128)(2,1)}), bf16[128,8192]{1,0:T(8,128)(2,1)}) %reduce-scatter.39.cloned.1.call-update) | async-done | bytes 2097168
  4885.3 33.8 all-gather.18
  (3710 shorter events, 2254.2 us)
Async XLA Ops:
  7.2 966.4 %copy-start = (bf16[4,448,512]{2,1,0:T(8,128)(2,1)S(1)}, bf16[4,448,512]{2,1,0:T(8,128)(2,1)}, u32[]{:S(2)}) copy-start(bf16[4,448,512]{2,1,0:T(8,128)(2,1)} %param.28) | copy-start | bytes 5505028
  7.2 138.7 %all-gather.32.cloned.1.call-start = ((), (), s32[]{:S(2)}) async-start(), calls=%async_computation.12 | async-start | bytes 10485760 | tf_op jit(solution)/shard_map/all_gather | solution.py:169
  8.1 773.9 %copy-start.40 = (f32[14,128]{1,0:T(8,128)}, f32[14,128]{1,0:T(8,128)S(1)}, u32[]{:S(2)}) copy-start(f32[14,128]{1,0:T(8,128)S(1)} %convert_element_type.306) | copy-start | bytes 21508
  9.2 740.5 %copy-start.52 = (f32[128]{0:T(128)}, f32[128]{0:T(128)S(1)}, u32[]{:S(2)}) copy-start(f32[128]{0:T(128)S(1)} %get-tuple-element.1417) | copy-start | bytes 1540
  9.2 740.5 %copy-start.54 = (f32[128]{0:T(128)}, f32[128]{0:T(128)S(1)}, u32[]{:S(2)}) copy-start(f32[128]{0:T(128)S(1)} %get-tuple-element.1418) | copy-start | bytes 1540
  9.2 1507.9 %copy-start.34 = (f32[4,128]{1,0:T(4,128)}, f32[4,128]{1,0:T(4,128)S(1)}, u32[]{:S(2)}) copy-start(f32[4,128]{1,0:T(4,128)S(1)} %broadcast_subtract_fusion.4) | copy-start | bytes 6148
  87.5 353.8 %reduce-scatter.17.cloned.1.call-start = ((), (), s32[]{:S(2)}) async-start(), calls=%async_computation.13 | async-start | bytes 20971520 | tf_op jit(solution)/shard_map/reduce_scatter | solution.py:177
  160.8 615.0 %all-gather.42.cloned.1.call-start = ((), (), s32[]{:S(2)}) async-start(), calls=%async_computation.27 | async-start | bytes 2621440 | tf_op jit(solution)/shard_map/all_gather | solution.py:169
  161.8 283.1 %copy-start.59 = (f32[2,64]{1,0:T(2,128)}, f32[2,64]{1,0:T(2,128)S(1)}, u32[]{:S(2)}) copy-start(f32[2,64]{1,0:T(2,128)S(1)} %exp.150) | copy-start | bytes 1540
  752.4 105.3 %reduce-scatter.19.cloned.1.call-start = ((), (), s32[]{:S(2)}) async-start(), calls=%async_computation.14 | async-start | bytes 5242880 | tf_op jit(solution)/shard_map/reduce_scatter | solution.py:177
  780.7 189.8 %all-gather.34.cloned.1.call-start = ((), (), s32[]{:S(2)}) async-start(), calls=%async_computation.15 | async-start | bytes 5242880 | tf_op jit(solution)/shard_map/all_gather | solution.py:169
  936.3 362.5 %reduce-scatter.21.cloned.1.call-start = ((), (), s32[]{:S(2)}) async-start(), calls=%async_computation.16 | async-start | bytes 23592960 | tf_op jit(solution)/shard_map/reduce_scatter | solution.py:177
  984.9 371.2 %all-gather.44.cloned.1.call-start = ((), (), s32[]{:S(2)}) async-start(), calls=%async_computation.28 | async-start | bytes 9175040 | tf_op jit(solution)/shard_map/all_gather | solution.py:169
  1302.6 140.1 %reduce-scatter.23.cloned.1.call-start = ((), (), s32[]{:S(2)}) async-start(), calls=%async_computation.17 | async-start | bytes 5242880 | tf_op jit(solution)/shard_map/reduce_scatter | solution.py:177
  1365.8 213.4 %all-gather.36.cloned.1.call-start = ((), (), s32[]{:S(2)}) async-start(), calls=%async_computation.18 | async-start | bytes 10485760 | tf_op jit(solution)/shard_map/all_gather | solution.py:169
  1365.9 1342.8 %copy-start.2 = (f32[2048,128]{0,1:T(8,128)}, f32[2048,128]{0,1:T(8,128)S(1)}, u32[]{:S(2)}) copy-start(f32[2048,128]{0,1:T(8,128)S(1)} %convert_bitcast_fusion) | copy-start | bytes 3145732
  1520.5 354.1 %reduce-scatter.25.cloned.1.call-start = ((), (), s32[]{:S(2)}) async-start(), calls=%async_computation.19 | async-start | bytes 20971520 | tf_op jit(solution)/shard_map/reduce_scatter | solution.py:177
  1594.1 1032.7 %all-gather.46.cloned.1.call-start = ((), (), s32[]{:S(2)}) async-start(), calls=%async_computation.29 | async-start | bytes 2621440 | tf_op jit(solution)/shard_map/all_gather | solution.py:169
  2603.4 105.3 %reduce-scatter.27.cloned.1.call-start = ((), (), s32[]{:S(2)}) async-start(), calls=%async_computation.20 | async-start | bytes 5242880 | tf_op jit(solution)/shard_map/reduce_scatter | solution.py:177
  2631.8 189.4 %all-gather.38.cloned.1.call-start = ((), (), s32[]{:S(2)}) async-start(), calls=%async_computation.21 | async-start | bytes 5242880 | tf_op jit(solution)/shard_map/all_gather | solution.py:169
  2787.1 362.4 %reduce-scatter.29.cloned.1.call-start = ((), (), s32[]{:S(2)}) async-start(), calls=%async_computation.22 | async-start | bytes 23592960 | tf_op jit(solution)/shard_map/reduce_scatter | solution.py:177
  2835.5 371.2 %all-gather.50.cloned.1.call-start = ((), (), s32[]{:S(2)}) async-start(), calls=%async_computation.31 | async-start | bytes 9175040 | tf_op jit(solution)/shard_map/all_gather | solution.py:169
  3153.2 140.0 %reduce-scatter.33.cloned.1.call-start = ((), (), s32[]{:S(2)}) async-start(), calls=%async_computation.24 | async-start | bytes 5242880 | tf_op jit(solution)/shard_map/reduce_scatter | solution.py:177
  3216.3 126.7 %all-gather.48.cloned.1.call-start = ((), (), s32[]{:S(2)}) async-start(), calls=%async_computation.30 | async-start | bytes 2621440 | tf_op jit(solution)/shard_map/all_gather | solution.py:182
  3296.3 120.1 %reduce-scatter.31.cloned.1.call-start = ((), (), s32[]{:S(2)}) async-start(), calls=%async_computation.23 | async-start | bytes 9175040 | tf_op jit(solution)/shard_map/reduce_scatter | solution.py:200
  3352.1 236.3 %all-gather.40.cloned.1.call-start = ((), (), s32[]{:S(2)}) async-start(), calls=%async_computation.25 | async-start | bytes 11796480 | tf_op jit(solution)/shard_map/all_gather | solution.py:182
  3421.4 238.8 %reduce-scatter.37.cloned.1.call-start = ((), (), s32[]{:S(2)}) async-start(), calls=%async_computation.34 | async-start | bytes 5242880
  3617.3 141.4 %all-gather.52.cloned.1.call-start = ((), (), s32[]{:S(2)}) async-start(), calls=%async_computation.32 | async-start | bytes 2621440 | tf_op jit(solution)/shard_map/all_gather | solution.py:182
  3714.9 78.4 %reduce-scatter.35.cloned.1.call-start = ((), (), s32[]{:S(2)}) async-start(), calls=%async_computation.26 | async-start | bytes 2621440 | tf_op jit(solution)/shard_map/reduce_scatter | solution.py:200
  3763.0 844.7 %all-gather.54.cloned.1.call-start = ((), (), s32[]{:S(2)}) async-start(), calls=%async_computation.33 | async-start | bytes 10485760 | tf_op jit(solution)/shard_map/all_gather | solution.py:182
  4457.8 331.3 %all-reduce.17.cloned.1.call-start = ((), (), s32[]{:S(2)}) async-start(), calls=%async_computation.36 | async-start | bytes 13631488 | tf_op jit(solution)/shard_map/psum | solution.py:342
  4623.8 239.7 %reduce-scatter.39.cloned.1.call-start = ((), (), s32[]{:S(2)}) async-start(), calls=%async_computation.35 | async-start | bytes 10485760
  (85 other events, 1632.2 us)
Sparse Core Ops, SparseCore 0:
  87.6 58.2 all-gather.31
  160.9 280.2 reduce-scatter.16
  752.5 23.2 all-gather.41
  780.8 76.7 reduce-scatter.18
  936.5 33.9 all-gather.33
  985.0 313.7 reduce-scatter.20
  1302.7 53.3 all-gather.43
  1365.9 76.7 reduce-scatter.22
  1520.7 58.4 all-gather.35
  1594.2 280.2 reduce-scatter.24
  2603.5 23.3 all-gather.45
  2631.9 76.7 reduce-scatter.26
  2787.2 33.9 all-gather.37
  2835.7 313.7 reduce-scatter.28
  3153.3 53.3 all-gather.49
  3216.4 76.7 reduce-scatter.32
  3296.4 46.4 all-gather.47
  3352.2 64.1 reduce-scatter.30
  3421.5 166.7 all-gather.39
  3617.4 42.6 reduce-scatter.36
  3715.0 43.6 all-gather.51
  3763.1 30.1 reduce-scatter.34
  4458.0 149.6 all-gather.53
  4623.9 165.1 all-reduce.16
  4791.7 71.7 reduce-scatter.38
